TPU v7x, 256 devices: a whole 4x4x8 slice. The times are simulated.
256 devices in a mesh: group: 2 (over z_lo), inner: 128 (over x, z_hi, y, core).
Axes of the slice: x: 4, y: 4, z: 8 (z_hi: 4, z_lo: 2; z = z_hi * 2 + z_lo), core: 2. Of those that a mesh axis runs over, the one named last changes fastest.
Arguments:
- voltages: bfloat16 [128, 768, 2, 16, 128], P('inner', 'group'), may hold values from -7 to 7
- coeffs: float32 [3, 16, 128], replicated, may hold values from -2 to 2
Outputs:
- autos: float32 [128, 2, 768, 384], P('inner', None, 'group')
- cross: float32 [128, 2, 384, 384], P('inner', None, 'group')
All inputs are finite; a program needn't handle non-finite values.
Results may differ from a plain program's by a relative error of at most 0.0025.
Values may be sent and summed in bfloat16 or wider, within the bound.
A program may use at most 320 MiB of HBM per device.

v0:
```python
import math

import jax
import jax.numpy as jnp
import numpy as np
from jax import lax
from jax.sharding import PartitionSpec as P

SUBCHANNELS = 16
TAPS = 3


def passed_along(x, axis, by):
    devices = lax.axis_size(axis)
    pairs = [(i, i + by) for i in range(devices) if 0 <= i + by < devices]
    return lax.ppermute(x, axis, pairs)


def partner(x, axis, distance):
    return lax.ppermute(x, axis, [(i, i ^ 1 << distance) for i in range(lax.axis_size(axis))])


def dft_block(length_dft):
    indices = np.arange(length_dft)
    angles = 2.0 * np.pi * (indices[:, None] * indices[None, :] % length_dft) / length_dft
    cosine = np.cos(angles)
    sine_table = np.sin(angles)
    upper = np.stack([cosine, -sine_table], axis=1)
    lower = np.stack([sine_table, cosine], axis=1)
    return np.stack([upper, lower], axis=0)


def twiddle_tables(channel_count):
    fine_count = SUBCHANNELS * channel_count
    rows_k = np.arange(SUBCHANNELS)[:, None]
    cols_q = np.arange(channel_count)[None, :]
    angles = 2.0 * np.pi * (rows_k * cols_q % fine_count) / fine_count
    factor = 1.0 / math.sqrt(fine_count)
    return (np.cos(angles) * factor, np.sin(angles) * factor)


def filterbank(extended, coeffs, frame_count):
    history_len = TAPS - 1
    channel_count = extended.shape[-1]
    accumulated = jnp.zeros((frame_count,) + extended.shape[1:], jnp.float32)
    for tap_index in range(TAPS):
        window = extended[history_len - tap_index : history_len - tap_index + frame_count].astype(
            jnp.float32
        )
        accumulated = accumulated + coeffs[tap_index] * window
    filtered = accumulated.astype(jnp.bfloat16)
    inputs_count = filtered.shape[1]
    flat_in = filtered.reshape(frame_count, inputs_count, 2 * SUBCHANNELS, channel_count)
    first_table = jnp.asarray(
        dft_block(SUBCHANNELS).reshape(2 * SUBCHANNELS, 2 * SUBCHANNELS), jnp.float32
    ).astype(jnp.bfloat16)
    section_one = jnp.einsum(
        "fixq,xy->fiyq", flat_in, first_table, preferred_element_type=jnp.float32
    )
    section_one = section_one.reshape(frame_count, inputs_count, 2, SUBCHANNELS, channel_count)
    real_part = section_one[:, :, 0]
    imag_part = section_one[:, :, 1]
    cos_np, sin_np = twiddle_tables(channel_count)
    cosine_tw = jnp.asarray(cos_np, jnp.float32)
    sine_tw = jnp.asarray(sin_np, jnp.float32)
    tw_real = real_part * cosine_tw + imag_part * sine_tw
    tw_imag = imag_part * cosine_tw - real_part * sine_tw
    twisted = jnp.stack([tw_real, tw_imag], axis=3).astype(jnp.bfloat16)
    twisted = twisted.reshape(frame_count, inputs_count, SUBCHANNELS, 2 * channel_count)
    second_table = jnp.asarray(
        dft_block(channel_count).reshape(2 * channel_count, 2, channel_count), jnp.float32
    ).astype(jnp.bfloat16)
    spectra = jnp.einsum(
        "fiks,srm->mfkri", twisted, second_table, preferred_element_type=jnp.float32
    )
    return spectra.astype(jnp.bfloat16)


def correlate_block(row_source, column_source):
    flipped = jnp.stack([row_source[:, :, :, 1], -row_source[:, :, :, 0]], axis=3)
    chan_count = row_source.shape[0]
    stacked = jnp.stack([row_source, flipped], 1).reshape(chan_count, 2, -1, row_source.shape[4])
    flat_columns = column_source.reshape(chan_count, -1, column_source.shape[4])
    return jnp.einsum("crsa,csb->crab", stacked, flat_columns, preferred_element_type=jnp.float32)


def shards(voltages, coeffs):
    history_len = TAPS - 1
    frame_count = voltages.shape[0]
    distances = (history_len + frame_count - 1) // frame_count
    received = []
    for distance in range(1, distances + 1):
        wanted = min(frame_count, history_len - (distance - 1) * frame_count)
        received.append(passed_along(voltages, "inner", distance))
    extended = jnp.concatenate(received[::-1] + [voltages], 0)
    spectra = filterbank(extended, coeffs, frame_count)
    turned = lax.all_to_all(spectra, "inner", split_axis=0, concat_axis=1, tiled=True)
    total_frames = turned.shape[1]
    scale_factor = 1.0 / (total_frames * SUBCHANNELS)
    autos = correlate_block(turned, turned) * scale_factor
    group_index = lax.axis_index("group")
    half_frames = total_frames // 2
    mine_half = lax.dynamic_slice_in_dim(turned, group_index * half_frames, half_frames, axis=1)
    send_half = lax.dynamic_slice_in_dim(
        turned, (1 - group_index) * half_frames, half_frames, axis=1
    )
    incoming = partner(send_half, "group", 0)
    row_source = jnp.where(group_index == 1, mine_half, incoming)
    column_source = jnp.where(group_index == 0, mine_half, incoming)
    partial_value = correlate_block(row_source, column_source) * scale_factor
    cross = lax.psum_scatter(partial_value, "group", scatter_dimension=2, tiled=True)
    return (autos, cross)


def solution(mesh):
    placed = (P("inner", "group", None, None, None), P())
    return jax.shard_map(
        shards,
        mesh=mesh,
        in_specs=placed,
        out_specs=(P("inner", None, "group", None), P("inner", None, "group", None)),
        check_vma=False,
    )
```

profile of v0, /device:TPU:17, one launch (start us, length us, event | category | flops | bytes accessed | tf_op | source)
XLA Modules:
  0.0 460.4 jit_solution(14531227364476569472)
XLA Ops:
  7.2 3.5 collective-permute-start
  10.6 4.6 collective-permute-start.1
  15.9 60.3 %collective-permute-done = bf16[1,384,2,16,128]{4,3,2,1,0:T(8,128)(2,1)S(1)} collective-permute-done((bf16[1,384,2,16,128]{4,3,2,1,0:T(8,128)(2,1)}, bf16[1,384,2,16,128]{4,3,2,1,0:T(8,128)(2,1)S(1)}, u32[]{:S(2)}, u32[]{:S(2)}) %collective-permute-start) | collective-permute-done | bytes 3145760 | tf_op jit(solution)/shard_map/ppermute | solution.py:16
  76.3 37.1 %collective-permute-done.1 = bf16[1,384,2,16,128]{4,3,2,1,0:T(8,128)(2,1)S(1)} collective-permute-done((bf16[1,384,2,16,128]{4,3,2,1,0:T(8,128)(2,1)}, bf16[1,384,2,16,128]{4,3,2,1,0:T(8,128)(2,1)S(1)}, u32[]{:S(2)}, u32[]{:S(2)}) %collective-permute-start.1) | collective-permute-done | bytes 3145760 | tf_op jit(solution)/shard_map/ppermute | solution.py:16
  113.4 3.7 add_convert_fusion
  119.2 4.9 %copy.40 = bf16[1,384,16,2,128]{4,3,1,2,0:T(2,128)(2,1)} copy(bf16[1,384,16,2,128]{4,2,1,3,0:T(8,128)(2,1)S(1)} %pad_maximum_fusion) | data formatting | bytes 6291456 | tf_op jit(solution)/shard_map/stack | solution.py:68
  124.1 4.6 reshape.159
  128.7 2.6 convert_bitcast_fusion
  131.4 8.8 %copy.41 = bf16[128,1,16,2,384]{4,3,2,1,0:T(2,128)(2,1)} copy(bf16[128,1,16,2,384]{0,4,3,2,1:T(8,128)(2,1)} %convert_bitcast_fusion) | data formatting | bytes 6291456 | tf_op jit(solution)/shard_map/convert_element_type | solution.py:76
  140.2 117.6 %all-to-all-start = ((bf16[128,1,16,2,384]{4,3,2,1,0:T(2,128)(2,1)}), bf16[128,1,16,2,384]{4,3,2,1,0:T(2,128)(2,1)S(1)}, u32[]{:S(2)}, u32[]{:S(2)}) async-start(bf16[128,1,16,2,384]{4,3,2,1,0:T(2,128)(2,1)} %copy.41), calls=%async_computation | async-start | bytes 6291456 | tf_op jit(solution)/shard_map/all_to_all | solution.py:97
  258.0 73.4 %all-to-all-done = bf16[128,1,16,2,384]{4,3,2,1,0:T(2,128)(2,1)S(1)} async-done(((bf16[128,1,16,2,384]{4,3,2,1,0:T(2,128)(2,1)}), bf16[128,1,16,2,384]{4,3,2,1,0:T(2,128)(2,1)S(1)}, u32[]{:S(2)}, u32[]{:S(2)}) %all-to-all-start) | async-done | bytes 3145760 | tf_op jit(solution)/shard_map/all_to_all | solution.py:97
  331.4 3.3 constant_dynamic-slice_fusion.1
  334.7 1.4 copy.61
  336.1 35.8 %collective-permute-done.2 = bf16[1,64,16,2,384]{4,2,3,1,0:T(8,128)(2,1)} collective-permute-done((bf16[1,64,16,2,384]{4,2,3,1,0:T(8,128)(2,1)}, bf16[1,64,16,2,384]{4,2,3,1,0:T(8,128)(2,1)}, u32[]{:S(2)}, u32[]{:S(2)}) %collective-permute-start.2) | collective-permute-done | bytes 1572896 | tf_op jit(solution)/shard_map/ppermute | solution.py:20
  372.0 3.5 broadcast_select_fusion.1
  375.6 2.4 copy.46
  378.1 2.4 copy.47
  380.5 4.7 %stack.38 = bf16[1,1,2048,384]{3,2,1,0:T(8,128)(2,1)} reshape(bf16[1,64,16,2,384]{4,3,2,1,0:T(2,128)(2,1)} %copy.47) | data formatting | bytes 3145728 | tf_op jit(solution)/shard_map/stack | solution.py:82
  385.2 2.7 copy.49
  387.9 4.7 %stack.36 = bf16[1,1,2048,384]{3,2,1,0:T(8,128)(2,1)} reshape(bf16[1,64,16,2,384]{4,3,2,1,0:T(2,128)(2,1)} %copy.46) | data formatting | bytes 3145728 | tf_op jit(solution)/shard_map/stack | solution.py:82
  392.5 2.7 copy.48
  395.2 3.8 copy.50
  399.0 4.7 %reshape.162 = bf16[2048,384,1]{1,0,2:T(8,128)(2,1)} reshape(bf16[1,64,16,2,384]{4,3,2,1,0:T(2,128)(2,1)} %copy.50) | data formatting | bytes 3145728 | tf_op jit(solution)/shard_map/reshape.31
  403.7 5.2 %fusion.13 = f32[1,2,384,384]{3,2,1,0:T(8,128)} fusion(bf16[2048,384,1]{1,0,2:T(8,128)(2,1)} %reshape.162, bf16[1,1,2048,384]{2,3,1,0:T(8,128)(2,1)} %copy.49, bf16[1,1,2048,384]{2,3,1,0:T(8,128)(2,1)} %copy.48), kind=kOutput, calls=%fused_computation.27 | convolution fusion | flops 1209827328 | bytes 5898240 | tf_op jit(solution)/shard_map/crsa,csb->crab/dot_general | solution.py:84
  408.9 5.8 %fusion.16 = (bf16[1,128,16,1,384]{4,3,2,1,0:T(2,128)(2,1)S(1)}, bf16[1,128,16,1,384]{4,3,2,1,0:T(2,128)(2,1)S(1)}) fusion(bf16[1,128,16,2,384]{4,3,2,1,0:T(2,128)(2,1)S(1)} %bitcast.74), kind=kLoop, calls=%fused_computation.36 | loop fusion | flops 786432 | bytes 6291456 | tf_op jit(solution)/shard_map/slice | solution.py:80
  414.7 8.1 %pad_maximum_fusion.1 = bf16[1,128,16,2,384]{4,3,2,1,0:T(2,128)(2,1)} fusion(bf16[1,128,16,1,384]{4,3,2,1,0:T(2,128)(2,1)S(1)} %get-tuple-element.9, bf16[1,128,16,1,384]{4,3,2,1,0:T(2,128)(2,1)S(1)} %get-tuple-element.8), kind=kLoop, calls=%fused_computation.9 | loop fusion | flops 6291456 | bytes 6291456 | tf_op jit(solution)/shard_map/stack | solution.py:80
  422.8 7.6 %stack.34 = bf16[1,1,4096,384]{3,2,1,0:T(8,128)(2,1)} reshape(bf16[1,128,16,2,384]{4,3,2,1,0:T(2,128)(2,1)} %pad_maximum_fusion.1) | data formatting | bytes 6291456 | tf_op jit(solution)/shard_map/stack | solution.py:82
  430.3 4.7 %copy.43 = bf16[1,1,4096,384]{2,3,1,0:T(8,128)(2,1)} copy(bf16[1,1,4096,384]{3,2,1,0:T(8,128)(2,1)} %stack.34) | data formatting | bytes 6291456 | tf_op jit(solution)/shard_map/stack | solution.py:82
  435.1 2.8 stack.32
  437.8 4.8 %copy.42 = bf16[1,1,4096,384]{2,3,1,0:T(8,128)(2,1)} copy(bf16[1,1,4096,384]{3,2,1,0:T(8,128)(2,1)} %stack.32) | data formatting | bytes 6291456 | tf_op jit(solution)/shard_map/stack | solution.py:82
  442.6 2.8 reshape.161
  445.4 8.2 %fusion.11 = f32[1,2,384,384]{3,2,1,0:T(8,128)} fusion(bf16[4096,384,1]{1,0,2:T(8,128)(2,1)} %reshape.161, bf16[1,1,4096,384]{2,3,1,0:T(8,128)(2,1)} %copy.43, bf16[1,1,4096,384]{2,3,1,0:T(8,128)(2,1)} %copy.42), kind=kOutput, calls=%fused_computation.25 | convolution fusion | flops 2419359744 | bytes 10616832 | tf_op jit(solution)/shard_map/crsa,csb->crab/dot_general | solution.py:84
  (18 shorter events, 3.4 us)
Async XLA Ops:
  7.2 69.1 %collective-permute-start = (bf16[1,384,2,16,128]{4,3,2,1,0:T(8,128)(2,1)}, bf16[1,384,2,16,128]{4,3,2,1,0:T(8,128)(2,1)S(1)}, u32[]{:S(2)}, u32[]{:S(2)}) collective-permute-start(bf16[1,384,2,16,128]{4,3,2,1,0:T(8,128)(2,1)} %param.6), channel_id=1, source_target_pairs={{0,1},{1,2},{2,3},{3,4},{4,5},{5,6},{6,7},{7,8},{8,9},{9,10},{10,1... | collective-permute-start | bytes 9437192 | tf_op jit(solution)/shard_map/ppermute | solution.py:16
  10.6 102.7 %collective-permute-start.1 = (bf16[1,384,2,16,128]{4,3,2,1,0:T(8,128)(2,1)}, bf16[1,384,2,16,128]{4,3,2,1,0:T(8,128)(2,1)S(1)}, u32[]{:S(2)}, u32[]{:S(2)}) collective-permute-start(bf16[1,384,2,16,128]{4,3,2,1,0:T(8,128)(2,1)} %param.6), channel_id=1, source_target_pairs={{0,2},{1,3},{2,4},{3,5},{4,6},{5,7},{6,8},{7,9},{8,10},{9,11},{10,... | collective-permute-start | bytes 9437192 | tf_op jit(solution)/shard_map/ppermute | solution.py:16
  113.4 3.7 copy-start.3
  117.1 1.0 copy-start.1
  117.1 1.0 copy-start.2
  124.1 4.6 %copy-start = (bf16[256,2,128,1]{2,0,1,3:T(8,128)(2,1)S(1)}, bf16[256,2,128,1]{2,0,1,3:T(8,128)(2,1)}, u32[]{:S(2)}) copy-start(bf16[256,2,128,1]{2,0,1,3:T(8,128)(2,1)} %constant.34) | copy-start | bytes 393220
  140.2 191.2 %all-to-all-start = ((bf16[128,1,16,2,384]{4,3,2,1,0:T(2,128)(2,1)}), bf16[128,1,16,2,384]{4,3,2,1,0:T(2,128)(2,1)S(1)}, u32[]{:S(2)}, u32[]{:S(2)}) async-start(bf16[128,1,16,2,384]{4,3,2,1,0:T(2,128)(2,1)} %copy.41), calls=%async_computation | async-start | bytes 6291456 | tf_op jit(solution)/shard_map/all_to_all | solution.py:97
  257.8 195.8 %reduce-scatter.2.cloned.1.call-start = ((), (), s32[]{:S(2)}) async-start(), calls=%async_computation.2 | async-start | bytes 1769472 | tf_op jit(solution)/shard_map/reduce_scatter | solution.py:111
  336.1 35.8 %collective-permute-start.2 = (bf16[1,64,16,2,384]{4,2,3,1,0:T(8,128)(2,1)}, bf16[1,64,16,2,384]{4,2,3,1,0:T(8,128)(2,1)}, u32[]{:S(2)}, u32[]{:S(2)}) collective-permute-start(bf16[1,64,16,2,384]{4,2,3,1,0:T(8,128)(2,1)} %bitcast.73), channel_id=1, source_target_pairs={{0,128},{128,0},{1,129},{129,1},{2,130},{130,2},{3,131},{131,3},{4... | collective-permute-start | bytes 4718600 | tf_op jit(solution)/shard_map/ppermute | solution.py:20
Sparse Core Ops, SparseCore 0:
  409.0 23.0 reduce-scatter.1
where the time goes:
time: 465 us; the launch traced here: 460 us
  waiting for transfers between devices  207 us (45%)
  starting transfers between devices  126 us (27%)
  local copies, waits for them, and re-layouts  74.3 us (16%)
  other arithmetic  22.5 us (5%)
  matrix products  16.9 us (4%)
  between operations  14.2 us (3%)
    all_to_all x1, starting transfers between devices, shards(): lax.all_to_all(spectra, 'inner', split_axis=0, concat_axis=1, tiled=True)  118 us
    ppermute x2, waiting for transfers between devices, passed_along(): return lax.ppermute(x, axis, pairs)  97.4 us
    all_to_all x1, waiting for transfers between devices, shards(): lax.all_to_all(spectra, 'inner', split_axis=0, concat_axis=1, tiled=True)  73.4 us
    ppermute x1, waiting for transfers between devices, partner(): lax.ppermute(x, axis, [(i, i ^ 1 << distance) for i in range(lax.axis_siz...  35.8 us
    another operation x8, local copies, waits for them, and re-layouts, correlate_block(): jnp.stack([row_source, flipped], 1)  34.5 us
    dot_general x2, matrix products, correlate_block(): jnp.einsum('crsa,csb->crab', stacked, flat_columns, preferred_element_typ...  13.3 us
  transfers between devices with their start and end apart: 5, of which 4 were waited for; matrix products, arithmetic and copies ran while one was open for 10% of the time, Pallas kernels for 0%

commit v1 on v0

--- a/solution.py
+++ b/solution.py
@@ -1,10 +1,15 @@
+import functools
 import math
 
 import jax
 import jax.numpy as jnp
 import numpy as np
 from jax import lax
+from jax.experimental import pallas as pl
+from jax.experimental.pallas import tpu as pltpu
 from jax.sharding import PartitionSpec as P
+
+MESH_ID = pl.DeviceIdType.MESH
 
 SUBCHANNELS = 16
 TAPS = 3
@@ -84,6 +89,52 @@
     return jnp.einsum("crsa,csb->crab", stacked, flat_columns, preferred_element_type=jnp.float32)
 
 
+def turn_kernel(count, src, dst, send_sem, recv_sem, own_sem):
+    me = lax.axis_index("inner")
+    barrier = pltpu.get_barrier_semaphore()
+
+    def greet(step, carry):
+        pl.semaphore_signal(
+            barrier, inc=1, device_id={"inner": lax.rem(me + step, count)}, device_id_type=MESH_ID
+        )
+        return carry
+
+    lax.fori_loop(1, count, greet, 0)
+    own = pltpu.make_async_copy(src.at[me], dst.at[me], own_sem)
+    own.start()
+    pl.semaphore_wait(barrier, count - 1)
+
+    def send(step, carry):
+        peer = lax.rem(me + step, count)
+        pltpu.make_async_remote_copy(
+            src_ref=src.at[peer],
+            dst_ref=dst.at[me],
+            send_sem=send_sem,
+            recv_sem=recv_sem,
+            device_id={"inner": peer},
+            device_id_type=MESH_ID,
+        ).start()
+        return carry
+
+    lax.fori_loop(1, count, send, 0)
+    own.wait()
+    rest = pl.ds(0, count - 1)
+    pltpu.make_async_copy(src.at[rest], dst.at[rest], send_sem).wait()
+    pltpu.make_async_copy(src.at[rest], dst.at[rest], recv_sem).wait()
+
+
+def corner_turn(spectra):
+    count = spectra.shape[0]
+    return pl.pallas_call(
+        functools.partial(turn_kernel, count),
+        out_shape=jax.ShapeDtypeStruct(spectra.shape, spectra.dtype),
+        in_specs=[pl.BlockSpec(memory_space=pltpu.VMEM)],
+        out_specs=pl.BlockSpec(memory_space=pltpu.VMEM),
+        scratch_shapes=[pltpu.SemaphoreType.DMA] * 3,
+        compiler_params=pltpu.CompilerParams(collective_id=0, has_side_effects=True),
+    )(spectra)
+
+
 def shards(voltages, coeffs):
     history_len = TAPS - 1
     frame_count = voltages.shape[0]
@@ -94,7 +145,9 @@
         received.append(passed_along(voltages, "inner", distance))
     extended = jnp.concatenate(received[::-1] + [voltages], 0)
     spectra = filterbank(extended, coeffs, frame_count)
-    turned = lax.all_to_all(spectra, "inner", split_axis=0, concat_axis=1, tiled=True)
+    chan_count = spectra.shape[0]
+    rows = spectra.reshape(chan_count, 2 * SUBCHANNELS * frame_count, spectra.shape[-1])
+    turned = corner_turn(rows).reshape(1, chan_count * frame_count, SUBCHANNELS, 2, -1)
     total_frames = turned.shape[1]
     scale_factor = 1.0 / (total_frames * SUBCHANNELS)
     autos = correlate_block(turned, turned) * scale_factor

time: 465 us -> 452 us (0.972)
  Pallas kernels: 0 us -> 188 us
  starting transfers between devices: 126 us -> 8.08 us
  waiting for transfers between devices: 207 us -> 134 us
  local copies, waits for them, and re-layouts: 74.3 us -> 54.7 us
  other arithmetic: 22.5 us -> 33.6 us
    pallas_call x0 -> x1, Pallas kernels: none -> 188 us  [corner_turn(): pl.pallas_call(functools.partial(turn_kernel, count), out_shape=jax.Shape...]
    all_to_all x1 -> x0, starting transfers between devices: 118 us -> none  [shards(): lax.all_to_all(spectra, 'inner', split_axis=0, concat_axis=1, tiled=True)]
    all_to_all x1 -> x0, waiting for transfers between devices: 73.4 us -> none  [shards(): lax.all_to_all(spectra, 'inner', split_axis=0, concat_axis=1, tiled=True)]
    reshape x0 -> x2, local copies, waits for them, and re-layouts: none -> 11.1 us  [the longest x1 6.09 us: shards(): corner_turn(rows).reshape(1, chan_count * frame_count, SUBCHANNELS, 2, -1)]
    another operation x8 -> x7, local copies, waits for them, and re-layouts: 34.5 us -> 25.2 us  [correlate_block(): jnp.stack([row_source, flipped], 1)]
    convert_element_type x1 -> x0, local copies, waits for them, and re-layouts: 8.79 us -> none  [filterbank(): return spectra.astype(jnp.bfloat16)]
    select_n x2 -> x0, local copies, waits for them, and re-layouts: 6.23 us -> none  [the longest x1 3.83 us: shards(): column_source = jnp.where(group_index == 0, mine_half, incoming)]
    another operation x3 -> x1, local copies, waits for them, and re-layouts: 9.82 us -> 4.66 us
  transfers between devices with their start and end apart: 5 -> 4, of which waited for: 4 -> 3; matrix products, arithmetic and copies ran while one was open for 10% -> 7% of each run, Pallas kernels for 0% -> 0%
where the time goes in v1:
time: 452 us; the launch traced here: 449 us
  Pallas kernels  188 us (42%)
  waiting for transfers between devices  134 us (30%)
  local copies, waits for them, and re-layouts  54.7 us (12%)
  other arithmetic  33.6 us (7%)
  matrix products  16 us (4%)
  between operations  14.2 us (3%)
  starting transfers between devices  8.08 us (2%)
    pallas_call x1, Pallas kernels, corner_turn(): pl.pallas_call(functools.partial(turn_kernel, count), out_shape=jax.Shape...  188 us
    ppermute x2, waiting for transfers between devices, passed_along(): return lax.ppermute(x, axis, pairs)  97.5 us
    ppermute x1, waiting for transfers between devices, partner(): lax.ppermute(x, axis, [(i, i ^ 1 << distance) for i in range(lax.axis_siz...  36.2 us
    another operation x7, local copies, waits for them, and re-layouts, correlate_block(): jnp.stack([row_source, flipped], 1)  25.2 us
    another operation x2, other arithmetic, correlate_block(): jnp.stack([row_source[:, :, :, 1], -row_source[:, :, :, 0]], axis=3)  13.1 us
    dot_general x2, matrix products, correlate_block(): jnp.einsum('crsa,csb->crab', stacked, flat_columns, preferred_element_typ...  12.4 us
    slice x2, other arithmetic, correlate_block(): row_source[:, :, :, 1]  9.8 us
  transfers between devices with their start and end apart: 4, of which 3 were waited for; matrix products, arithmetic and copies ran while one was open for 7% of the time, Pallas kernels for 0%

profile of v1, /device:TPU:17, one launch (start us, length us, event | category | flops | bytes accessed | tf_op | source)
XLA Modules:
  0.0 448.6 jit_solution(2182668332385304362)
XLA Ops:
  7.2 3.5 collective-permute-start
  10.7 4.6 %collective-permute-start.1 = (bf16[1,384,2,16,128]{4,3,2,1,0:T(8,128)(2,1)}, bf16[1,384,2,16,128]{4,3,2,1,0:T(8,128)(2,1)}, u32[]{:S(2)}, u32[]{:S(2)}) collective-permute-start(bf16[1,384,2,16,128]{4,3,2,1,0:T(8,128)(2,1)} %param.6), channel_id=1, source_target_pairs={{0,2},{1,3},{2,4},{3,5},{4,6},{5,7},{6,8},{7,9},{8,10},{9,11},{10,... | collective-permute-start | bytes 9437192 | tf_op jit(solution)/shard_map/ppermute | solution.py:21
  15.3 0.7 slice_bitcast_fusion.4
  16.0 60.3 %collective-permute-done = bf16[1,384,2,16,128]{4,3,2,1,0:T(8,128)(2,1)S(1)} collective-permute-done((bf16[1,384,2,16,128]{4,3,2,1,0:T(8,128)(2,1)}, bf16[1,384,2,16,128]{4,3,2,1,0:T(8,128)(2,1)S(1)}, u32[]{:S(2)}, u32[]{:S(2)}) %collective-permute-start) | collective-permute-done | bytes 3145760 | tf_op jit(solution)/shard_map/ppermute | solution.py:21
  76.3 37.2 %collective-permute-done.1 = bf16[1,384,2,16,128]{4,3,2,1,0:T(8,128)(2,1)} collective-permute-done((bf16[1,384,2,16,128]{4,3,2,1,0:T(8,128)(2,1)}, bf16[1,384,2,16,128]{4,3,2,1,0:T(8,128)(2,1)}, u32[]{:S(2)}, u32[]{:S(2)}) %collective-permute-start.1) | collective-permute-done | bytes 3145760 | tf_op jit(solution)/shard_map/ppermute | solution.py:21
  113.5 4.7 %add_convert_fusion = bf16[1,384,2,16,128]{4,3,2,1,0:T(8,128)(2,1)S(1)} fusion(bf16[1,384,2,16,128]{4,3,2,1,0:T(8,128)(2,1)} %collective-permute-done.1, bf16[1,384,2,16,128]{4,3,2,1,0:T(8,128)(2,1)S(1)} %collective-permute-done, bf16[1,384,2,16,128]{4,3,2,1,0:T(8,128)(2,1)} %param.6, f32[16,128]{1,0:T(8,128)S(1)} %get-tuple-element.11, ...), kind=kLoop, calls=%fused_computation.4 | loop fusion | flops 14155776 | bytes 12607488 | tf_op jit(solution)/shard_map/convert_element_type | solution.py:56
  118.2 1.0 fusion.19
  119.2 0.8 add_convert_fusion.1
  120.3 4.9 %copy.16 = bf16[1,384,16,2,128]{4,3,1,2,0:T(2,128)(2,1)} copy(bf16[1,384,16,2,128]{4,2,1,3,0:T(8,128)(2,1)S(1)} %pad_maximum_fusion) | data formatting | bytes 6291456 | tf_op jit(solution)/shard_map/stack | solution.py:73
  125.2 4.6 %reshape.158 = bf16[384,16,256,1]{2,0,1,3:T(8,128)(2,1)S(1)} reshape(bf16[1,384,16,2,128]{4,3,1,2,0:T(2,128)(2,1)} %copy.16) | data formatting | bytes 6291456 | tf_op jit(solution)/shard_map/convert_element_type | solution.py:73
  129.8 2.6 fusion.8
  132.4 5.0 %copy.23.src = bf16[128,32,384]{2,1,0:T(8,128)(2,1)} copy(bf16[128,32,384]{0,2,1:T(8,128)(2,1)} %bitcast.72) | data formatting | bytes 6291456 | tf_op jit(solution)/shard_map/reshape | solution.py:149
  137.5 188.4 %shard_map.77 = bf16[128,32,384]{2,1,0:T(8,128)(2,1)} custom-call(bf16[128,32,384]{2,1,0:T(8,128)(2,1)} %copy.23.src), custom_call_target="tpu_custom_call" | custom-call | tf_op jit(solution)/shard_map/pallas_call | solution.py:128
  325.9 6.1 %reshape.152 = bf16[1,128,16,2,384]{4,3,2,1,0:T(2,128)(2,1)S(1)} reshape(bf16[128,32,384]{2,1,0:T(8,128)(2,1)} %shard_map.77) | data formatting | bytes 6291456 | tf_op jit(solution)/shard_map/reshape | solution.py:150
  332.0 2.2 constant_dynamic-slice_fusion
  334.3 36.2 %collective-permute-done.2 = bf16[1,64,16,2,384]{4,3,2,1,0:T(2,128)(2,1)} collective-permute-done((bf16[1,64,16,2,384]{4,3,2,1,0:T(2,128)(2,1)}, bf16[1,64,16,2,384]{4,3,2,1,0:T(2,128)(2,1)}, u32[]{:S(2)}, u32[]{:S(2)}) %collective-permute-start.2) | collective-permute-done | bytes 1572896 | tf_op jit(solution)/shard_map/ppermute | solution.py:25
  370.4 4.9 %broadcast_select_fusion.1 = (bf16[1,64,16,2,384]{4,3,2,1,0:T(2,128)(2,1)S(1)}, bf16[1,64,16,2,384]{4,3,2,1,0:T(2,128)(2,1)}) fusion(bf16[1,64,16,2,384]{4,3,2,1,0:T(2,128)(2,1)} %collective-permute-done.2, pred[]{:T(512)S(6)} %eq.6, bf16[1,128,16,2,384]{4,3,2,1,0:T(2,128)(2,1)S(1)} %reshape.152, s32[]{:T(128)S(6)} %select_n.21, pred[]{:T(512)S(6)} %eq.7), kind=kLoop, calls=%fused_computation.19 | loop fusion | flops 1572864 | bytes 6291462 | tf_op jit(solution)/shard_map/jit(_where)/select_n | solution.py:161
  375.3 1.1 copy-done.1
  376.4 4.0 fusion.18
  380.5 4.7 %stack.35 = bf16[1,1,2048,384]{3,2,1,0:T(8,128)(2,1)} reshape(bf16[1,64,16,2,384]{4,3,2,1,0:T(2,128)(2,1)} %copy-done.1) | data formatting | bytes 3145728 | tf_op jit(solution)/shard_map/stack | solution.py:87
  385.1 5.6 %pad_maximum_fusion.2 = bf16[1,64,16,2,384]{4,3,2,1,0:T(2,128)(2,1)} fusion(bf16[1,64,16,1,384]{4,3,2,1,0:T(2,128)(2,1)} %get-tuple-element.9, bf16[1,64,16,1,384]{4,3,2,1,0:T(2,128)(2,1)} %get-tuple-element.8), kind=kLoop, calls=%fused_computation.22 | loop fusion | flops 3145728 | bytes 3145728 | tf_op jit(solution)/shard_map/stack | solution.py:85
  390.7 4.7 %stack.37 = bf16[1,1,2048,384]{3,2,1,0:T(8,128)(2,1)} reshape(bf16[1,64,16,2,384]{4,3,2,1,0:T(2,128)(2,1)} %pad_maximum_fusion.2) | data formatting | bytes 3145728 | tf_op jit(solution)/shard_map/stack | solution.py:87
  395.4 2.6 copy.21
  398.0 2.7 copy.20
  400.7 4.7 %reshape.161 = bf16[2048,384,1]{1,0,2:T(8,128)(2,1)} reshape(bf16[1,64,16,2,384]{4,3,2,1,0:T(2,128)(2,1)} %get-tuple-element.5) | data formatting | bytes 3145728 | tf_op jit(solution)/shard_map/reshape.25
  405.4 5.2 %fusion.14 = f32[1,2,384,384]{3,2,1,0:T(8,128)} fusion(bf16[2048,384,1]{1,0,2:T(8,128)(2,1)} %reshape.161, bf16[1,1,2048,384]{2,3,1,0:T(8,128)(2,1)} %copy.21, bf16[1,1,2048,384]{2,3,1,0:T(8,128)(2,1)} %copy.20), kind=kOutput, calls=%fused_computation.26 | convolution fusion | flops 1209827328 | bytes 5898240 | tf_op jit(solution)/shard_map/crsa,csb->crab/dot_general | solution.py:89
  410.6 5.8 %fusion.17 = (bf16[1,128,16,1,384]{4,3,2,1,0:T(2,128)(2,1)S(1)}, bf16[1,128,16,1,384]{4,3,2,1,0:T(2,128)(2,1)S(1)}) fusion(bf16[1,128,16,2,384]{4,3,2,1,0:T(2,128)(2,1)S(1)} %reshape.152), kind=kLoop, calls=%fused_computation.33 | loop fusion | flops 786432 | bytes 6291456 | tf_op jit(solution)/shard_map/slice | solution.py:85
  416.3 7.5 %pad_maximum_fusion.1 = bf16[1,128,16,2,384]{4,3,2,1,0:T(2,128)(2,1)S(1)} fusion(bf16[1,128,16,1,384]{4,3,2,1,0:T(2,128)(2,1)S(1)} %get-tuple-element.7, bf16[1,128,16,1,384]{4,3,2,1,0:T(2,128)(2,1)S(1)} %get-tuple-element.6), kind=kLoop, calls=%fused_computation.9 | loop fusion | flops 6291456 | bytes 6291456 | tf_op jit(solution)/shard_map/stack | solution.py:85
  423.8 2.8 stack.33
  426.6 4.9 %copy.19 = bf16[1,1,4096,384]{2,3,1,0:T(8,128)(2,1)} copy(bf16[1,1,4096,384]{3,2,1,0:T(8,128)(2,1)} %stack.33) | data formatting | bytes 6291456 | tf_op jit(solution)/shard_map/stack | solution.py:87
  431.5 2.9 copy.18
  434.5 7.3 %fusion.12 = f32[1,2,384,384]{3,2,1,0:T(8,128)} fusion(bf16[4096,384,1]{1,0,2:T(8,128)(2,1)S(1)} %bitcast.70, bf16[1,1,4096,384]{2,3,1,0:T(8,128)(2,1)} %copy.19, bf16[1,1,4096,384]{2,3,1,0:T(8,128)(2,1)} %copy.18), kind=kOutput, calls=%fused_computation.24 | convolution fusion | flops 2419359744 | bytes 10616832 | tf_op jit(solution)/shard_map/crsa,csb->crab/dot_general | solution.py:89
  (16 shorter events, 0.4 us)
Async XLA Ops:
  7.2 434.6 %reduce-scatter.2.cloned.1.call-start = ((), (), s32[]{:S(2)}) async-start(), calls=%async_computation.1 | async-start | bytes 1769472 | tf_op jit(solution)/shard_map/reduce_scatter | solution.py:164
  7.2 69.1 %collective-permute-start = (bf16[1,384,2,16,128]{4,3,2,1,0:T(8,128)(2,1)}, bf16[1,384,2,16,128]{4,3,2,1,0:T(8,128)(2,1)S(1)}, u32[]{:S(2)}, u32[]{:S(2)}) collective-permute-start(bf16[1,384,2,16,128]{4,3,2,1,0:T(8,128)(2,1)} %param.6), channel_id=1, source_target_pairs={{0,1},{1,2},{2,3},{3,4},{4,5},{5,6},{6,7},{7,8},{8,9},{9,10},{10,1... | collective-permute-start | bytes 9437192 | tf_op jit(solution)/shard_map/ppermute | solution.py:21
  10.7 102.8 %collective-permute-start.1 = (bf16[1,384,2,16,128]{4,3,2,1,0:T(8,128)(2,1)}, bf16[1,384,2,16,128]{4,3,2,1,0:T(8,128)(2,1)}, u32[]{:S(2)}, u32[]{:S(2)}) collective-permute-start(bf16[1,384,2,16,128]{4,3,2,1,0:T(8,128)(2,1)} %param.6), channel_id=1, source_target_pairs={{0,2},{1,3},{2,4},{3,5},{4,6},{5,7},{6,8},{7,9},{8,10},{9,11},{10,... | collective-permute-start | bytes 9437192 | tf_op jit(solution)/shard_map/ppermute | solution.py:21
  113.5 4.7 %copy-start.5 = (bf16[32,32,1]{0,1,2:T(8,128)(2,1)S(1)}, bf16[32,32,1]{0,1,2:T(8,128)(2,1)}, u32[]{:S(2)}) copy-start(bf16[32,32,1]{0,1,2:T(8,128)(2,1)} %constant.31) | copy-start | bytes 6148
  118.2 1.0 copy-start.3
  118.2 1.0 copy-start.4
  125.2 4.6 %copy-start.2 = (bf16[256,2,128,1]{2,0,1,3:T(8,128)(2,1)S(1)}, bf16[256,2,128,1]{2,0,1,3:T(8,128)(2,1)}, u32[]{:S(2)}) copy-start(bf16[256,2,128,1]{2,0,1,3:T(8,128)(2,1)} %constant.32) | copy-start | bytes 393220
  334.3 36.2 %collective-permute-start.2 = (bf16[1,64,16,2,384]{4,3,2,1,0:T(2,128)(2,1)}, bf16[1,64,16,2,384]{4,3,2,1,0:T(2,128)(2,1)}, u32[]{:S(2)}, u32[]{:S(2)}) collective-permute-start(bf16[1,64,16,2,384]{4,3,2,1,0:T(2,128)(2,1)} %constant_dynamic-slice_fusion), channel_id=1, source_target_pairs={{0,128},{128,0},{1,129},{129,1},{2,130},{130,2},{3,131},{131,3},{4... | collective-permute-start | bytes 4718600 | tf_op jit(solution)/shard_map/ppermute | solution.py:25
  375.3 1.1 copy-start.1
  426.6 4.9 %copy-start = (bf16[128,32,384]{2,1,0:T(8,128)(2,1)S(1)}, bf16[128,32,384]{2,1,0:T(8,128)(2,1)}, u32[]{:S(2)}) copy-start(bf16[128,32,384]{2,1,0:T(8,128)(2,1)} %shard_map.77) | copy-start | bytes 9437188
Sparse Core Ops, SparseCore 0:
  410.7 29.8 reduce-scatter.1

commit v2 on v0

v2 whole, which is shorter than its diff:
```python
import functools
import math

import jax
import jax.numpy as jnp
import numpy as np
from jax import lax
from jax.experimental import pallas as pl
from jax.experimental.pallas import tpu as pltpu
from jax.sharding import PartitionSpec as P

MESH_ID = pl.DeviceIdType.MESH
SUBCHANNELS = 16
TAPS = 3
CHANNELS = 128
RING = 8
BLOCKS = 16
ZS = 4
XS = 4
HISTORY = TAPS - 1
LANES = 128
CHUNK = 16


def dft_block(length_dft):
    indices = np.arange(length_dft)
    angles = 2.0 * np.pi * (indices[:, None] * indices[None, :] % length_dft) / length_dft
    cosine = np.cos(angles)
    sine_table = np.sin(angles)
    upper = np.stack([cosine, -sine_table], axis=1)
    lower = np.stack([sine_table, cosine], axis=1)
    return np.stack([upper, lower], axis=0)


def twiddle_tables(channel_count):
    fine_count = SUBCHANNELS * channel_count
    rows_k = np.arange(SUBCHANNELS)[:, None]
    cols_q = np.arange(channel_count)[None, :]
    angles = 2.0 * np.pi * (rows_k * cols_q % fine_count) / fine_count
    factor = 1.0 / math.sqrt(fine_count)
    return (np.cos(angles) * factor, np.sin(angles) * factor)


def tables():
    small = dft_block(SUBCHANNELS)
    first = np.einsum("fg,rpsk->sfkgrp", np.eye(RING), small)
    rows = RING * 2 * SUBCHANNELS
    first = first.reshape(rows, rows)
    second = dft_block(CHANNELS).reshape(2 * CHANNELS, 2 * CHANNELS).T
    order = np.einsum("ij,mn->mijn", np.eye(CHUNK), np.eye(CHUNK))
    order = order.reshape(CHUNK * CHUNK, CHUNK * CHUNK)
    cos_np, sin_np = twiddle_tables(CHANNELS)
    as_bf16 = [jnp.asarray(t, jnp.float32).astype(jnp.bfloat16) for t in (first, second, order)]
    as_f32 = [jnp.asarray(np.tile(t, (RING, 1)), jnp.float32) for t in (cos_np, sin_np)]
    return as_bf16 + as_f32


def ring_turn_kernel(per, volts, out, send_sem, recv_sem, halo_send, halo_recv):
    me = lax.axis_index("inner")
    count = lax.axis_size("inner")
    ring = lax.rem(me, RING)
    base = me - ring
    following = lax.rem(me + RING, count)
    previous = lax.rem(me + count - RING, count)
    tail = ring // (RING - HISTORY)
    chunks = per // CHUNK
    barrier = pltpu.get_barrier_semaphore()
    peers = [base + lax.rem(ring + s, RING) for s in range(1, RING)]
    for peer in peers + [following, previous]:
        pl.semaphore_signal(barrier, inc=1, device_id={"inner": peer}, device_id_type=MESH_ID)
    pl.semaphore_wait(barrier, RING + 1)
    for k in range(chunks):
        part = pl.ds(k * CHUNK, CHUNK)
        for s in range(1, RING):
            owner = lax.rem(ring + s, RING)
            pltpu.make_async_remote_copy(
                src_ref=volts.at[pl.ds(owner * per + k * CHUNK, CHUNK)],
                dst_ref=out.at[HISTORY + ring, part],
                send_sem=send_sem,
                recv_sem=recv_sem.at[k, tail],
                device_id={"inner": base + owner},
                device_id_type=MESH_ID,
            ).start()
        pltpu.make_async_copy(
            volts.at[pl.ds(ring * per + k * CHUNK, CHUNK)],
            out.at[HISTORY + ring, part],
            recv_sem.at[k, tail],
        ).start()
    for k in range(chunks):
        part = pl.ds(k * CHUNK, CHUNK)
        last = out.at[pl.ds(RING, HISTORY), part]
        first = out.at[pl.ds(0, HISTORY), part]
        pltpu.make_async_copy(last, last, recv_sem.at[k, 1]).wait()
        pltpu.make_async_remote_copy(
            src_ref=last,
            dst_ref=first,
            send_sem=halo_send,
            recv_sem=halo_recv.at[k],
            device_id={"inner": following},
            device_id_type=MESH_ID,
        ).start()
    for k in range(chunks):
        part = pl.ds(k * CHUNK, CHUNK)
        early = out.at[pl.ds(HISTORY, RING - HISTORY), part]
        pltpu.make_async_copy(early, early, recv_sem.at[k, 0]).wait()
        first = out.at[pl.ds(0, HISTORY), part]
        pltpu.make_async_copy(first, first, halo_recv.at[k]).wait()
    sent = volts.at[pl.ds(0, (RING - 1) * per)]
    pltpu.make_async_copy(sent, sent, send_sem).wait()
    first = out.at[pl.ds(0, HISTORY)]
    pltpu.make_async_copy(first, first, halo_send).wait()

    @pl.when(me < RING)
    def _():
        out[0:HISTORY] = jnp.zeros((HISTORY,) + out.shape[1:], out.dtype)


def ring_turn(volts):
    inputs = volts.shape[0]
    per = inputs // RING
    chunks = per // CHUNK
    return pl.pallas_call(
        functools.partial(ring_turn_kernel, per),
        out_shape=jax.ShapeDtypeStruct((RING + HISTORY, per) + volts.shape[1:], volts.dtype),
        in_specs=[pl.BlockSpec(memory_space=pl.ANY)],
        out_specs=pl.BlockSpec(memory_space=pltpu.VMEM),
        scratch_shapes=[
            pltpu.SemaphoreType.DMA,
            pltpu.SemaphoreType.DMA((chunks, 2)),
            pltpu.SemaphoreType.DMA,
            pltpu.SemaphoreType.DMA((chunks,)),
        ],
        compiler_params=pltpu.CompilerParams(collective_id=0, has_side_effects=True),
    )(volts)


def spectra_chunk(k, frames, coeffs, first, second, order, cosine, sine, stage, out):
    half = CHANNELS
    taps = [jnp.concatenate([coeffs[t], coeffs[t]], 0) for t in range(TAPS)]

    def pair(step, carry):
        sections = []
        for j in range(2):
            source = k * CHUNK + step * 2 + j
            held = [frames[t, source].astype(jnp.float32) for t in range(RING + HISTORY)]
            rows = []
            for t in range(RING):
                total = taps[0] * held[t + HISTORY]
                for tap in range(1, TAPS):
                    total = total + taps[tap] * held[t + HISTORY - tap]
                rows.append(total.astype(jnp.bfloat16))
            sections.append(jnp.concatenate(rows, 0))
        filtered = jnp.concatenate(sections, 1)
        one = jnp.dot(first[...], filtered, preferred_element_type=jnp.float32)
        cos_tw = cosine[...]
        sin_tw = sine[...]
        twisted = []
        for j in range(2):
            lanes = slice(j * LANES, (j + 1) * LANES)
            real = one[:half, lanes]
            imag = one[half:, lanes]
            tw_real = real * cos_tw + imag * sin_tw
            tw_imag = imag * cos_tw - real * sin_tw
            twisted.append(jnp.concatenate([tw_real, tw_imag], 1).astype(jnp.bfloat16))
        spectra = lax.dot_general(
            second[...],
            jnp.concatenate(twisted, 0),
            (((1,), (1,)), ((), ())),
            preferred_element_type=jnp.float32,
        ).astype(jnp.bfloat16)
        for j in range(2):
            rows = pl.ds(pl.multiple_of((step * 2 + j) * CHUNK, CHUNK), CHUNK)
            for part in range(2):
                for group in range(CHANNELS // CHUNK):
                    start = part * CHANNELS + group * CHUNK
                    stage[group, rows, part * LANES : (part + 1) * LANES] = spectra[
                        start : start + CHUNK, j * LANES : (j + 1) * LANES
                    ]
        return carry

    lax.fori_loop(0, CHUNK // 2, pair, 0)

    def turn(group, carry):
        turned = jnp.dot(order[...], stage[group], preferred_element_type=jnp.float32)
        turned = turned.astype(jnp.bfloat16).reshape(CHUNK, CHUNK, 2 * LANES)
        out[k, pl.ds(group * CHUNK, CHUNK)] = turned
        return carry

    lax.fori_loop(0, CHANNELS // CHUNK, turn, 0)


def spectra_kernel(frames, coeffs, first, second, order, cosine, sine, out, stage):
    for k in range(out.shape[0]):
        spectra_chunk(k, frames, coeffs, first, second, order, cosine, sine, stage, out)


def make_spectra(frames, coeffs, constants):
    per = frames.shape[1]
    vmem = pl.BlockSpec(memory_space=pltpu.VMEM)
    return pl.pallas_call(
        spectra_kernel,
        out_shape=jax.ShapeDtypeStruct(
            (per // CHUNK, CHANNELS, CHUNK, 2 * LANES), jnp.bfloat16
        ),
        in_specs=[vmem] * 7,
        out_specs=vmem,
        scratch_shapes=[pltpu.VMEM((CHANNELS // CHUNK, CHUNK * CHUNK, 2 * LANES), jnp.bfloat16)],
    )(frames, coeffs, *constants)


def correlate(rows, columns, total):
    depth = rows.shape[-1]
    pieces = []
    for start in range(0, depth, 2 * LANES):
        pieces.append(rows[:, start + LANES : start + 2 * LANES])
        pieces.append(-rows[:, start : start + LANES])
    flipped = jnp.concatenate(pieces, 1)
    contract = (((1,), (1,)), ((), ()))
    total[0] += lax.dot_general(rows, columns, contract, preferred_element_type=jnp.float32)
    total[1] += lax.dot_general(flipped, columns, contract, preferred_element_type=jnp.float32)


def corner_kernel(
    spectra,
    autos,
    cross,
    held,
    partial,
    incoming,
    send_sem,
    recv_sem,
    cross_sem,
    forward_sem,
    sum_sem,
    own_sem,
):
    me = lax.axis_index("inner")
    group = lax.axis_index("group")
    other = 1 - group
    ring = lax.rem(me, RING)
    zee = lax.rem(me // RING, ZS)
    ex = me // (RING * ZS)
    towards = 2 * group - 1
    plane = RING * XS
    parts = spectra.shape[0]
    inputs = parts * CHUNK * RING

    def place(step, zed):
        x_to = lax.rem(ex + step // RING, XS)
        ring_to = lax.rem(ring + lax.rem(step, RING), RING)
        return (x_to * ZS + zed) * RING + ring_to

    def at_distance(distance):
        return lax.rem(zee + distance + 2 * ZS, ZS)

    barrier = pltpu.get_barrier_semaphore()

    def greet(group_to, zed, begin):
        def body(step, carry):
            pl.semaphore_signal(
                barrier,
                inc=1,
                device_id={"group": group_to, "inner": place(step, zed)},
                device_id_type=MESH_ID,
            )
            return carry

        lax.fori_loop(begin, plane, body, 0)

    for distance in range(ZS):
        greet(group, at_distance(distance), 1 if distance == 0 else 0)
    greet(other, zee, 0)
    greet(other, at_distance(towards), 0)
    lanes_here = pl.ds(pl.multiple_of(ex * 2 * LANES, 2 * LANES), 2 * LANES)
    rows_here = pl.ds(ring * parts, parts)

    own = pltpu.make_async_copy(
        spectra.at[:, me], held.at[group, 0, rows_here, :, lanes_here], own_sem
    )
    own.start()
    autos[...] = jnp.zeros(autos.shape, autos.dtype)
    partial[...] = jnp.zeros(partial.shape, partial.dtype)
    pl.semaphore_wait(barrier, (ZS + 2) * plane - 1)

    def send(group_to, zed, begin, sem):
        slot = lax.rem(zee - zed + ZS, ZS)

        def body(step, carry):
            peer = place(step, zed)
            pltpu.make_async_remote_copy(
                src_ref=spectra.at[:, peer],
                dst_ref=held.at[group, slot, rows_here, :, lanes_here],
                send_sem=send_sem,
                recv_sem=sem.at[slot],
                device_id={"group": group_to, "inner": peer},
                device_id_type=MESH_ID,
            ).start()
            return carry

        lax.fori_loop(begin, plane, body, 0)

    send(group, at_distance(2), 0, recv_sem)
    send(group, zee, 1, recv_sem)

    @pl.when(ex // 2 == group)
    def _():
        send(other, zee, 0, cross_sem)

    send(group, at_distance(-towards), 0, recv_sem)
    send(other, at_distance(towards), 0, cross_sem)
    send(group, at_distance(towards), 0, recv_sem)

    near = lax.rem(towards + ZS, ZS)
    own_half = pl.ds(pl.multiple_of(group * 4 * LANES, 4 * LANES), 4 * LANES)
    other_half = pl.ds(pl.multiple_of(other * 4 * LANES, 4 * LANES), 4 * LANES)

    def arrived(ref, sem):
        pltpu.make_async_copy(ref, ref, sem).wait()

    def flat(slot, which, lanes=slice(None)):
        block = held[which, slot, :, :, lanes]
        return block.reshape(inputs, block.shape[-1])

    own.wait()
    arrived(spectra.at[:, pl.ds(0, plane - 1)], recv_sem.at[0])
    mine = flat(0, group)
    correlate(mine, mine, autos)
    arrived(held.at[other, 0, :, :, other_half], cross_sem.at[0])
    correlate(flat(0, 1, other_half), flat(0, 0, other_half), partial)
    arrived(held.at[group, 2], recv_sem.at[2])
    forward = pltpu.make_async_remote_copy(
        src_ref=held.at[group, 2, :, :, own_half],
        dst_ref=held.at[group, 2, :, :, own_half],
        send_sem=forward_sem.at[0],
        recv_sem=forward_sem.at[1],
        device_id={"group": other},
        device_id_type=MESH_ID,
    )
    forward.start()
    mine = flat(2, group)
    correlate(mine, mine, autos)
    arrived(held.at[group, near], recv_sem.at[near])
    mine = flat(near, group)
    correlate(mine, mine, autos)
    arrived(held.at[other, near], cross_sem.at[near])
    correlate(flat(near, 1), flat(near, 0), partial)
    arrived(held.at[other, 2, :, :, other_half], forward_sem.at[1])
    correlate(flat(2, 1, other_half), flat(2, 0, other_half), partial)
    keep = inputs // 2
    swap = pltpu.make_async_remote_copy(
        src_ref=partial.at[:, pl.ds(pl.multiple_of(other * keep, keep), keep)],
        dst_ref=incoming,
        send_sem=sum_sem.at[0],
        recv_sem=sum_sem.at[1],
        device_id={"group": other},
        device_id_type=MESH_ID,
    )
    swap.start()
    far = lax.rem(ZS - towards, ZS)
    arrived(held.at[group, far], recv_sem.at[far])
    mine = flat(far, group)
    correlate(mine, mine, autos)
    scale = 1.0 / (RING * BLOCKS * SUBCHANNELS)
    autos[...] = autos[...] * scale
    swap.wait()
    kept = partial[:, pl.ds(pl.multiple_of(group * keep, keep), keep)]
    cross[...] = (kept + incoming[...]) * scale
    arrived(spectra.at[:, pl.ds(0, ZS * plane - 1)], send_sem)
    arrived(spectra.at[:, pl.ds(0, plane)], send_sem)

    @pl.when(ex // 2 == group)
    def _():
        arrived(spectra.at[:, pl.ds(0, plane)], send_sem)

    forward.wait_send()


def corner(spectra):
    parts = spectra.shape[0]
    inputs = parts * CHUNK * RING
    vmem = pl.BlockSpec(memory_space=pltpu.VMEM)
    return pl.pallas_call(
        corner_kernel,
        out_shape=(
            jax.ShapeDtypeStruct((2, inputs, inputs), jnp.float32),
            jax.ShapeDtypeStruct((2, inputs // 2, inputs), jnp.float32),
        ),
        in_specs=[vmem],
        out_specs=(vmem, vmem),
        scratch_shapes=[
            pltpu.VMEM((2, ZS, parts * RING, CHUNK, XS * 2 * LANES), jnp.bfloat16),
            pltpu.VMEM((2, inputs, inputs), jnp.float32),
            pltpu.VMEM((2, inputs // 2, inputs), jnp.float32),
            pltpu.SemaphoreType.DMA,
            pltpu.SemaphoreType.DMA((ZS,)),
            pltpu.SemaphoreType.DMA((ZS,)),
            pltpu.SemaphoreType.DMA((2,)),
            pltpu.SemaphoreType.DMA((2,)),
            pltpu.SemaphoreType.DMA,
        ],
        compiler_params=pltpu.CompilerParams(collective_id=1, has_side_effects=True),
    )(spectra)


def shards(voltages, coeffs):
    volts = voltages.reshape(voltages.shape[1], 2 * SUBCHANNELS, CHANNELS)
    frames = ring_turn(volts)
    spectra = make_spectra(frames, coeffs, tables())
    autos, cross = corner(spectra)
    return (autos[None], cross[None])


def solution(mesh):
    placed = (P("inner", "group", None, None, None), P())
    return jax.shard_map(
        shards,
        mesh=mesh,
        in_specs=placed,
        out_specs=(P("inner", None, "group", None), P("inner", None, "group", None)),
        check_vma=False,
    )
```

time: 465 us -> 226 us (0.49)
  the two profiles are of different devices: /device:TPU:17 before, /device:TPU:64 now
where the time goes in v2:
time: 226 us
  Pallas kernels  221 us (98%)
  local copies, waits for them, and re-layouts  4.28 us (2%)
    pallas_call x1, Pallas kernels, corner(): pl.pallas_call(corner_kernel, out_shape=(jax.ShapeDtypeStruct((2, inputs,...  149 us
    pallas_call x1, Pallas kernels, ring_turn(): pl.pallas_call(functools.partial(ring_turn_kernel, per), out_shape=jax.Sh...  52.4 us
    pallas_call x1, Pallas kernels, make_spectra(): pl.pallas_call(spectra_kernel, out_shape=jax.ShapeDtypeStruct((per // CHU...  19.7 us

profile of v2, /device:TPU:64, one launch (start us, length us, event | category | flops | bytes accessed | tf_op | source)
XLA Modules:
  0.0 226.2 jit_solution(17329200868885048821)
XLA Ops:
  0.6 52.4 %shard_map.86.frames = bf16[10,48,32,128]{3,2,1,0:T(8,128)(2,1)} custom-call(bf16[384,32,128]{2,1,0:T(8,128)(2,1)} %bitcast.3), custom_call_target="tpu_custom_call" | custom-call | tf_op jit(solution)/shard_map/pallas_call | solution.py:122
  53.1 19.7 %shard_map.87.spectra = bf16[3,128,16,256]{3,2,1,0:T(8,128)(2,1)} custom-call(bf16[10,48,32,128]{3,2,1,0:T(8,128)(2,1)} %shard_map.86.frames, f32[3,16,128]{2,1,0:T(8,128)} %coeffs.1, bf16[256,256]{1,0:T(8,128)(2,1)} %constant.16.first, bf16[256,256]{1,0:T(8,128)(2,1)} %constant.17.second, bf16[256,256]{1,0:T(8,128)(2,1)} %constant.18.order, ...), custom_call_target="tpu_custom_call" | custom-call | tf_op jit(solution)/shard_map/pallas_call | solution.py:200
  72.8 149.1 %shard_map.88 = (f32[2,384,384]{2,1,0:T(8,128)}, f32[2,192,384]{2,1,0:T(8,128)}) custom-call(bf16[3,128,16,256]{3,2,1,0:T(8,128)(2,1)} %shard_map.87.spectra), custom_call_target="tpu_custom_call" | custom-call | tf_op jit(solution)/shard_map/pallas_call | solution.py:382
  221.9 2.4 %copy.11 = f32[1,2,384,384]{3,2,1,0:T(8,128)} copy(f32[1,2,384,384]{3,2,1,0:T(8,128)} %bitcast.4) | data formatting | bytes 2359296
  224.2 1.9 copy.12

commit v3 on v2

v3 whole, which is shorter than its diff:
```python
import functools
import math

import jax
import jax.numpy as jnp
import numpy as np
from jax import lax
from jax.experimental import pallas as pl
from jax.experimental.pallas import tpu as pltpu
from jax.sharding import PartitionSpec as P

MESH_ID = pl.DeviceIdType.MESH
SUBCHANNELS = 16
TAPS = 3
CHANNELS = 128
RING = 8
BLOCKS = 16
ZS = 4
XS = 4
HISTORY = TAPS - 1
LANES = 128
CHUNK = 16


def dft_block(length_dft):
    indices = np.arange(length_dft)
    angles = 2.0 * np.pi * (indices[:, None] * indices[None, :] % length_dft) / length_dft
    cosine = np.cos(angles)
    sine_table = np.sin(angles)
    upper = np.stack([cosine, -sine_table], axis=1)
    lower = np.stack([sine_table, cosine], axis=1)
    return np.stack([upper, lower], axis=0)


def twiddle_tables(channel_count):
    fine_count = SUBCHANNELS * channel_count
    rows_k = np.arange(SUBCHANNELS)[:, None]
    cols_q = np.arange(channel_count)[None, :]
    angles = 2.0 * np.pi * (rows_k * cols_q % fine_count) / fine_count
    factor = 1.0 / math.sqrt(fine_count)
    return (np.cos(angles) * factor, np.sin(angles) * factor)


def tables():
    small = dft_block(SUBCHANNELS)
    first = np.einsum("fg,rpsk->sfkgrp", np.eye(RING), small)
    rows = RING * 2 * SUBCHANNELS
    first = first.reshape(rows, rows)
    second = dft_block(CHANNELS).reshape(2 * CHANNELS, 2 * CHANNELS).T
    order = np.einsum("ij,mn->mijn", np.eye(CHUNK), np.eye(CHUNK))
    order = order.reshape(CHUNK * CHUNK, CHUNK * CHUNK)
    cos_np, sin_np = twiddle_tables(CHANNELS)
    as_bf16 = [jnp.asarray(t, jnp.float32).astype(jnp.bfloat16) for t in (first, second, order)]
    as_f32 = [jnp.asarray(np.tile(t, (RING, 1)), jnp.float32) for t in (cos_np, sin_np)]
    return as_bf16 + as_f32


def spectra_chunk(k, frames, coeffs, first, second, order, cosine, sine, stage, out):
    half = CHANNELS
    taps = [jnp.concatenate([coeffs[t], coeffs[t]], 0) for t in range(TAPS)]

    def pair(step, carry):
        sections = []
        for j in range(2):
            source = k * CHUNK + step * 2 + j
            held = [frames[t, source].astype(jnp.float32) for t in range(RING + HISTORY)]
            rows = []
            for t in range(RING):
                total = taps[0] * held[t + HISTORY]
                for tap in range(1, TAPS):
                    total = total + taps[tap] * held[t + HISTORY - tap]
                rows.append(total.astype(jnp.bfloat16))
            sections.append(jnp.concatenate(rows, 0))
        filtered = jnp.concatenate(sections, 1)
        one = jnp.dot(first[...], filtered, preferred_element_type=jnp.float32)
        cos_tw = cosine[...]
        sin_tw = sine[...]
        twisted = []
        for j in range(2):
            lanes = slice(j * LANES, (j + 1) * LANES)
            real = one[:half, lanes]
            imag = one[half:, lanes]
            tw_real = real * cos_tw + imag * sin_tw
            tw_imag = imag * cos_tw - real * sin_tw
            twisted.append(jnp.concatenate([tw_real, tw_imag], 1).astype(jnp.bfloat16))
        spectra = lax.dot_general(
            second[...],
            jnp.concatenate(twisted, 0),
            (((1,), (1,)), ((), ())),
            preferred_element_type=jnp.float32,
        ).astype(jnp.bfloat16)
        for j in range(2):
            rows = pl.ds(pl.multiple_of((step * 2 + j) * CHUNK, CHUNK), CHUNK)
            for part in range(2):
                for group in range(CHANNELS // CHUNK):
                    start = part * CHANNELS + group * CHUNK
                    stage[group, rows, part * LANES : (part + 1) * LANES] = spectra[
                        start : start + CHUNK, j * LANES : (j + 1) * LANES
                    ]
        return carry

    lax.fori_loop(0, CHUNK // 2, pair, 0)

    def turn(group, carry):
        turned = jnp.dot(order[...], stage[group], preferred_element_type=jnp.float32)
        turned = turned.astype(jnp.bfloat16).reshape(CHUNK, CHUNK, 2 * LANES)
        out[k, pl.ds(group * CHUNK, CHUNK)] = turned
        return carry

    lax.fori_loop(0, CHANNELS // CHUNK, turn, 0)


def correlate(rows, columns, total, row_start, column_start):
    pieces = []
    for start in range(0, rows.shape[1], 2 * LANES):
        pieces.append(rows[:, start + LANES : start + 2 * LANES])
        pieces.append(-rows[:, start : start + LANES])
    flipped = jnp.concatenate(pieces, 1)
    contract = (((1,), (1,)), ((), ()))
    row_range = slice(row_start, row_start + rows.shape[0])
    column_range = slice(column_start, column_start + columns.shape[0])
    for part, left in enumerate((rows, flipped)):
        total[part, row_range, column_range] += lax.dot_general(
            left, columns, contract, preferred_element_type=jnp.float32
        )


def whole_kernel(
    volts,
    coeffs,
    first,
    second,
    order,
    cosine,
    sine,
    autos,
    cross,
    frames,
    stage,
    spectra,
    held,
    partial,
    incoming,
    turn_send,
    turn_recv,
    halo_send,
    halo_recv,
    send_sem,
    recv_sem,
    cross_sem,
    pass_send,
    pass_recv,
    sum_sem,
):
    me = lax.axis_index("inner")
    group = lax.axis_index("group")
    count = lax.axis_size("inner")
    other = 1 - group
    ring = lax.rem(me, RING)
    base = me - ring
    following = lax.rem(me + RING, count)
    tail = ring // (RING - HISTORY)
    zee = lax.rem(me // RING, ZS)
    ex = me // (RING * ZS)
    towards = 2 * group - 1
    plane = RING * XS
    chunks = spectra.shape[0]
    near = lax.rem(towards + ZS, ZS)
    far = lax.rem(ZS - towards, ZS)
    my_half = ex // (XS // 2)
    crossing = lax.rem(my_half + group, 2)
    staying = 1 - crossing
    met = lax.rem(my_half + other, 2)

    def at_distance(distance):
        return lax.rem(zee + distance + 2 * ZS, ZS)

    def place(step, zed):
        x_to = lax.rem(ex + step // RING, XS)
        ring_to = lax.rem(ring + lax.rem(step, RING), RING)
        return (x_to * ZS + zed) * RING + ring_to

    def to_half(half):
        def locate(step, zed):
            x_to = half * (XS // 2) + step // RING
            ring_to = lax.rem(ring + lax.rem(step, RING), RING)
            return (x_to * ZS + zed) * RING + ring_to

        return locate

    def x_lanes(x, width=1):
        return pl.ds(pl.multiple_of(x * 2 * LANES, 2 * LANES), width * 2 * LANES)

    def half_lanes(half):
        return x_lanes(half * (XS // 2), XS // 2)

    def arrived(ref, sem):
        pltpu.make_async_copy(ref, ref, sem).wait()

    barrier = pltpu.get_barrier_semaphore()

    def greet(group_to, zed, begin):
        def body(step, carry):
            pl.semaphore_signal(
                barrier,
                inc=1,
                device_id={"group": group_to, "inner": place(step, zed)},
                device_id_type=MESH_ID,
            )
            return carry

        lax.fori_loop(begin, plane, body, 0)

    for distance in range(ZS):
        greet(group, at_distance(distance), 1 if distance == 0 else 0)
    greet(other, zee, 0)
    greet(other, at_distance(towards), 0)
    greet(other, at_distance(2), 0)
    pl.semaphore_wait(barrier, (ZS + 3) * plane - 1)

    for k in range(chunks):
        mine = pl.ds(k * CHUNK, CHUNK)
        for s in range(1, RING):
            owner = lax.rem(ring + s, RING)
            pltpu.make_async_remote_copy(
                src_ref=volts.at[pl.ds((k * RING + owner) * CHUNK, CHUNK)],
                dst_ref=frames.at[HISTORY + ring, mine],
                send_sem=turn_send,
                recv_sem=turn_recv.at[k, tail],
                device_id={"inner": base + owner},
                device_id_type=MESH_ID,
            ).start()
        pltpu.make_async_copy(
            volts.at[pl.ds((k * RING + ring) * CHUNK, CHUNK)],
            frames.at[HISTORY + ring, mine],
            turn_recv.at[k, tail],
        ).start()

    def send_halo(k):
        mine = pl.ds(k * CHUNK, CHUNK)
        last = frames.at[pl.ds(RING, HISTORY), mine]
        arrived(last, turn_recv.at[k, 1])
        pltpu.make_async_remote_copy(
            src_ref=last,
            dst_ref=frames.at[pl.ds(0, HISTORY), mine],
            send_sem=halo_send,
            recv_sem=halo_recv.at[k],
            device_id={"inner": following},
            device_id_type=MESH_ID,
        ).start()

    def channelize(k):
        mine = pl.ds(k * CHUNK, CHUNK)
        arrived(frames.at[pl.ds(HISTORY, RING - HISTORY), mine], turn_recv.at[k, 0])
        arrived(frames.at[pl.ds(0, HISTORY), mine], halo_recv.at[k])

        @pl.when(me < RING)
        def _():
            frames[0:HISTORY, mine] = jnp.zeros(
                (HISTORY, CHUNK) + frames.shape[2:], frames.dtype
            )

        spectra_chunk(k, frames, coeffs, first, second, order, cosine, sine, stage, spectra)

    def send_spectra(k):
        row = k * RING + ring

        def send(group_to, zed, locate, begin, end, sem):
            slot = lax.rem(zee - zed + ZS, ZS)

            def body(step, carry):
                peer = locate(step, zed)
                pltpu.make_async_remote_copy(
                    src_ref=spectra.at[k, peer],
                    dst_ref=held.at[group, slot, row, :, x_lanes(ex)],
                    send_sem=send_sem,
                    recv_sem=sem(slot),
                    device_id={"group": group_to, "inner": peer},
                    device_id_type=MESH_ID,
                ).start()
                return carry

            lax.fori_loop(begin, end, body, 0)

        def by_slot(slot):
            return recv_sem.at[slot, k]

        def by_source(slot):
            return cross_sem.at[slot, k, ex]

        send(other, at_distance(towards), place, 0, plane, by_source)
        send(other, at_distance(2), to_half(crossing), 0, plane // 2, by_source)
        send(group, at_distance(2), to_half(staying), 0, plane // 2, by_slot)
        send(group, at_distance(-towards), place, 0, plane, by_slot)
        send(other, zee, to_half(crossing), 0, plane // 2, by_source)
        send(group, zee, place, 1, plane, by_slot)
        pltpu.make_async_copy(
            spectra.at[k, me], held.at[group, 0, row, :, x_lanes(ex)], recv_sem.at[0, k]
        ).start()

    def chunk_rows(k):
        return pl.ds(k * RING, RING)

    def hand_on(k):
        for x in range(XS):
            here = lax.rem(ex + XS - x, XS)
            pass_on(k, near, here, recv_sem.at[near, k])
        for x in range(XS // 2):
            pass_on(k, 2, met * (XS // 2) + x, pass_recv.at[k])

    def pass_on(k, slot, x, sem):
        block = held.at[other, slot, chunk_rows(k), :, x_lanes(x)]
        arrived(block, cross_sem.at[slot, k, x])
        pltpu.make_async_remote_copy(
            src_ref=block,
            dst_ref=block,
            send_sem=pass_send,
            recv_sem=sem,
            device_id={"group": other},
            device_id_type=MESH_ID,
        ).start()

    def flat(which, slot, begin, end, lanes=slice(None)):
        block = held[which, slot, begin * RING : end * RING, :, lanes]
        return block.reshape((end - begin) * RING * CHUNK, block.shape[-1])

    size = RING * CHUNK

    def add_early(which_rows, which_columns, slot, total, lanes=slice(None)):
        last = chunks - 1
        rows = flat(which_rows, slot, 0, last, lanes)
        columns = flat(which_columns, slot, 0, last, lanes)
        correlate(rows, columns, total, 0, 0)

    def add_late(which_rows, which_columns, slot, total, lanes=slice(None)):
        last = chunks - 1
        columns = flat(which_columns, slot, 0, chunks, lanes)
        correlate(flat(which_rows, slot, last, chunks, lanes), columns, total, last * size, 0)
        correlate(
            flat(which_rows, slot, 0, last, lanes), columns[last * size :], total, 0, last * size
        )

    def wait_own(slot, k):
        arrived(held.at[group, slot, chunk_rows(k)], recv_sem.at[slot, k])

    def wait_staying(k):
        arrived(held.at[group, 2, chunk_rows(k), :, half_lanes(met)], recv_sem.at[2, k])

    def wait_passed(k):
        arrived(held.at[group, 2, chunk_rows(k), :, half_lanes(1 - met)], pass_recv.at[k])

    def wait_level(k):
        for x in range(XS // 2):
            here = met * (XS // 2) + x
            arrived(
                held.at[other, 0, chunk_rows(k), :, x_lanes(here)], cross_sem.at[0, k, here]
            )

    send_halo(0)
    send_halo(1)
    channelize(0)
    send_spectra(0)
    send_halo(2)
    channelize(1)
    send_spectra(1)
    hand_on(0)
    autos[...] = jnp.zeros(autos.shape, autos.dtype)
    partial[...] = jnp.zeros(partial.shape, partial.dtype)
    channelize(2)
    send_spectra(2)
    hand_on(1)
    for k in range(2):
        wait_own(0, k)
        wait_level(k)
    add_early(group, group, 0, autos)
    add_early(1, 0, 0, partial, half_lanes(met))
    hand_on(2)
    for k in range(2):
        wait_own(near, k)
    add_early(1, 0, near, partial)
    add_early(group, group, near, autos)
    for k in range(2):
        wait_staying(k)
    add_early(1, 0, 2, partial, half_lanes(met))
    for k in range(2):
        wait_passed(k)
    add_early(group, group, 2, autos)
    for k in range(2):
        wait_own(far, k)
    add_early(group, group, far, autos)
    wait_own(0, 2)
    wait_level(2)
    add_late(1, 0, 0, partial, half_lanes(met))
    wait_own(near, 2)
    add_late(1, 0, near, partial)
    wait_staying(2)
    add_late(1, 0, 2, partial, half_lanes(met))
    keep = chunks * size // 2
    swap = pltpu.make_async_remote_copy(
        src_ref=partial.at[:, pl.ds(pl.multiple_of(other * keep, keep), keep)],
        dst_ref=incoming,
        send_sem=sum_sem.at[0],
        recv_sem=sum_sem.at[1],
        device_id={"group": other},
        device_id_type=MESH_ID,
    )
    swap.start()
    add_late(group, group, 0, autos)
    add_late(group, group, near, autos)
    wait_passed(2)
    add_late(group, group, 2, autos)
    wait_own(far, 2)
    add_late(group, group, far, autos)
    swap.wait()
    cross[...] = partial[:, pl.ds(pl.multiple_of(group * keep, keep), keep)] + incoming[...]
    arrived(volts.at[pl.ds(0, (RING - 1) * chunks * CHUNK)], turn_send)
    arrived(frames.at[pl.ds(0, HISTORY)], halo_send)
    arrived(spectra.at[:, pl.ds(0, ZS * plane - 1)], send_sem)
    arrived(spectra.at[:, pl.ds(0, plane // 2)], send_sem)
    arrived(held.at[other, near], pass_send)
    arrived(held.at[other, 2, :, :, half_lanes(met)], pass_send)


def shards(voltages, coeffs):
    inputs = voltages.shape[1]
    volts = voltages.reshape(inputs, 2 * SUBCHANNELS, CHANNELS)
    chunks = inputs // (RING * CHUNK)
    vmem = pl.BlockSpec(memory_space=pltpu.VMEM)
    autos, cross = pl.pallas_call(
        whole_kernel,
        out_shape=(
            jax.ShapeDtypeStruct((2, inputs, inputs), jnp.float32),
            jax.ShapeDtypeStruct((2, inputs // 2, inputs), jnp.float32),
        ),
        in_specs=[pl.BlockSpec(memory_space=pl.ANY)] + [vmem] * 6,
        out_specs=(vmem, vmem),
        scratch_shapes=[
            pltpu.VMEM((RING + HISTORY, chunks * CHUNK) + volts.shape[1:], jnp.bfloat16),
            pltpu.VMEM((CHANNELS // CHUNK, CHUNK * CHUNK, 2 * LANES), jnp.bfloat16),
            pltpu.VMEM((chunks, CHANNELS, CHUNK, 2 * LANES), jnp.bfloat16),
            pltpu.VMEM((2, ZS, chunks * RING, CHUNK, XS * 2 * LANES), jnp.bfloat16),
            pltpu.VMEM((2, inputs, inputs), jnp.float32),
            pltpu.VMEM((2, inputs // 2, inputs), jnp.float32),
            pltpu.SemaphoreType.DMA,
            pltpu.SemaphoreType.DMA((chunks, 2)),
            pltpu.SemaphoreType.DMA,
            pltpu.SemaphoreType.DMA((chunks,)),
            pltpu.SemaphoreType.DMA,
            pltpu.SemaphoreType.DMA((ZS, chunks)),
            pltpu.SemaphoreType.DMA((ZS, chunks, XS)),
            pltpu.SemaphoreType.DMA,
            pltpu.SemaphoreType.DMA((chunks,)),
            pltpu.SemaphoreType.DMA((2,)),
        ],
        compiler_params=pltpu.CompilerParams(collective_id=0, has_side_effects=True),
    )(volts, coeffs, *tables())
    scale = 1.0 / (RING * BLOCKS * SUBCHANNELS)
    return (autos[None] * scale, cross[None] * scale)


def solution(mesh):
    placed = (P("inner", "group", None, None, None), P())
    return jax.shard_map(
        shards,
        mesh=mesh,
        in_specs=placed,
        out_specs=(P("inner", None, "group", None), P("inner", None, "group", None)),
        check_vma=False,
    )
```

time: 226 us -> 157 us (0.69)
  the two profiles are of different devices: /device:TPU:64 before, /device:TPU:17 now
where the time goes in v3:
time: 157 us
  Pallas kernels  153 us (97%)
  other arithmetic  3.28 us (2%)
    pallas_call x1, Pallas kernels, shards(): pl.pallas_call(whole_kernel, out_shape=(jax.ShapeDtypeStruct((2, inputs,...  153 us
    mul x2, other arithmetic, shards(): return (autos[None] * scale, cross[None] * scale)  3.28 us

profile of v3, /device:TPU:17, one launch (start us, length us, event | category | flops | bytes accessed | tf_op | source)
XLA Modules:
  0.0 157.1 jit_solution(13351396443329192944)
XLA Ops:
  0.6 153.2 %shard_map.86 = (f32[2,384,384]{2,1,0:T(8,128)}, f32[2,192,384]{2,1,0:T(8,128)}) custom-call(bf16[384,32,128]{2,1,0:T(8,128)(2,1)} %bitcast.5, f32[3,16,128]{2,1,0:T(8,128)} %coeffs.1, bf16[256,256]{1,0:T(8,128)(2,1)} %constant.19.first, bf16[256,256]{1,0:T(8,128)(2,1)} %constant.20.second, bf16[256,256]{1,0:T(8,128)(2,1)} %constant.21.order, ...), custom_call_target="tpu_custom_call" | custom-call | tf_op jit(solution)/shard_map/pallas_call | solution.py:429
  153.8 0.0 copy-start
  153.8 2.4 %multiply_bitcast_fusion = f32[1,2,384,384]{3,2,1,0:T(8,128)} fusion(f32[2,384,384]{2,1,0:T(8,128)} %get-tuple-element.4), kind=kLoop, calls=%fused_computation | loop fusion | flops 294912 | bytes 2359296 | tf_op jit(solution)/shard_map/mul | solution.py:458
  156.3 0.0 copy-done
  156.3 0.9 multiply_bitcast_fusion.1
Async XLA Ops:
  153.8 2.4 %copy-start = (f32[2,192,384]{2,1,0:T(8,128)S(1)}, f32[2,192,384]{2,1,0:T(8,128)}, u32[]{:S(2)}) copy-start(f32[2,192,384]{2,1,0:T(8,128)} %get-tuple-element.5) | copy-start | bytes 1769476

commit v4 on v3

--- a/solution.py
+++ b/solution.py
@@ -140,6 +140,7 @@
     spectra,
     held,
     partial,
+    outgoing,
     incoming,
     turn_send,
     turn_recv,
@@ -396,8 +397,10 @@
     wait_staying(2)
     add_late(1, 0, 2, partial, half_lanes(met))
     keep = chunks * size // 2
+    theirs = partial[:, pl.ds(pl.multiple_of(other * keep, keep), keep)]
+    outgoing[...] = theirs.astype(outgoing.dtype)
     swap = pltpu.make_async_remote_copy(
-        src_ref=partial.at[:, pl.ds(pl.multiple_of(other * keep, keep), keep)],
+        src_ref=outgoing,
         dst_ref=incoming,
         send_sem=sum_sem.at[0],
         recv_sem=sum_sem.at[1],
@@ -412,7 +415,8 @@
     wait_own(far, 2)
     add_late(group, group, far, autos)
     swap.wait()
-    cross[...] = partial[:, pl.ds(pl.multiple_of(group * keep, keep), keep)] + incoming[...]
+    kept = partial[:, pl.ds(pl.multiple_of(group * keep, keep), keep)]
+    cross[...] = kept + incoming[...].astype(jnp.float32)
     arrived(volts.at[pl.ds(0, (RING - 1) * chunks * CHUNK)], turn_send)
     arrived(frames.at[pl.ds(0, HISTORY)], halo_send)
     arrived(spectra.at[:, pl.ds(0, ZS * plane - 1)], send_sem)
@@ -440,7 +444,8 @@
             pltpu.VMEM((chunks, CHANNELS, CHUNK, 2 * LANES), jnp.bfloat16),
             pltpu.VMEM((2, ZS, chunks * RING, CHUNK, XS * 2 * LANES), jnp.bfloat16),
             pltpu.VMEM((2, inputs, inputs), jnp.float32),
-            pltpu.VMEM((2, inputs // 2, inputs), jnp.float32),
+            pltpu.VMEM((2, inputs // 2, inputs), jnp.bfloat16),
+            pltpu.VMEM((2, inputs // 2, inputs), jnp.bfloat16),
             pltpu.SemaphoreType.DMA,
             pltpu.SemaphoreType.DMA((chunks, 2)),
             pltpu.SemaphoreType.DMA,

time: 157 us -> 151 us (0.962)
  Pallas kernels: 153 us -> 147 us
    pallas_call x1, Pallas kernels: 153 us -> 147 us  [shards(): pl.pallas_call(whole_kernel, out_shape=(jax.ShapeDtypeStruct((2, inputs,...]
where the time goes in v4:
time: 151 us
  Pallas kernels  147 us (97%)
  other arithmetic  3.28 us (2%)
    pallas_call x1, Pallas kernels, shards(): pl.pallas_call(whole_kernel, out_shape=(jax.ShapeDtypeStruct((2, inputs,...  147 us
    mul x2, other arithmetic, shards(): return (autos[None] * scale, cross[None] * scale)  3.28 us

profile of v4, /device:TPU:17, one launch (start us, length us, event | category | flops | bytes accessed | tf_op | source)
XLA Modules:
  0.0 150.8 jit_solution(17114057923297298223)
XLA Ops:
  0.6 146.9 %shard_map.86 = (f32[2,384,384]{2,1,0:T(8,128)}, f32[2,192,384]{2,1,0:T(8,128)}) custom-call(bf16[384,32,128]{2,1,0:T(8,128)(2,1)} %bitcast.5, f32[3,16,128]{2,1,0:T(8,128)} %coeffs.1, bf16[256,256]{1,0:T(8,128)(2,1)} %constant.19.first, bf16[256,256]{1,0:T(8,128)(2,1)} %constant.20.second, bf16[256,256]{1,0:T(8,128)(2,1)} %constant.21.order, ...), custom_call_target="tpu_custom_call" | custom-call | tf_op jit(solution)/shard_map/pallas_call | solution.py:433
  147.5 0.0 copy-start
  147.5 2.4 %multiply_bitcast_fusion = f32[1,2,384,384]{3,2,1,0:T(8,128)} fusion(f32[2,384,384]{2,1,0:T(8,128)} %get-tuple-element.4), kind=kLoop, calls=%fused_computation | loop fusion | flops 294912 | bytes 2359296 | tf_op jit(solution)/shard_map/mul | solution.py:463
  149.9 0.0 copy-done
  149.9 0.9 multiply_bitcast_fusion.1
Async XLA Ops:
  147.5 2.4 %copy-start = (f32[2,192,384]{2,1,0:T(8,128)S(1)}, f32[2,192,384]{2,1,0:T(8,128)}, u32[]{:S(2)}) copy-start(f32[2,192,384]{2,1,0:T(8,128)} %get-tuple-element.5) | copy-start | bytes 1769476

commit v5 on v4

--- a/solution.py
+++ b/solution.py
@@ -152,6 +152,7 @@
     pass_send,
     pass_recv,
     sum_sem,
+    ready,
 ):
     me = lax.axis_index("inner")
     group = lax.axis_index("group")
@@ -199,27 +200,28 @@
         pltpu.make_async_copy(ref, ref, sem).wait()
 
     barrier = pltpu.get_barrier_semaphore()
-
-    def greet(group_to, zed, begin):
+    blocks = count // RING
+
+    def greet(group_to, begin):
         def body(step, carry):
             pl.semaphore_signal(
                 barrier,
                 inc=1,
-                device_id={"group": group_to, "inner": place(step, zed)},
+                device_id={"group": group_to, "inner": lax.rem(me + step * RING, count)},
                 device_id_type=MESH_ID,
             )
             return carry
 
-        lax.fori_loop(begin, plane, body, 0)
-
-    for distance in range(ZS):
-        greet(group, at_distance(distance), 1 if distance == 0 else 0)
-    greet(other, zee, 0)
-    greet(other, at_distance(towards), 0)
-    greet(other, at_distance(2), 0)
-    pl.semaphore_wait(barrier, (ZS + 3) * plane - 1)
-
-    for k in range(chunks):
+        lax.fori_loop(begin, blocks, body, 0)
+
+    mates = [base + lax.rem(ring + s, RING) for s in range(1, RING)]
+    for mate in mates:
+        pl.semaphore_signal(barrier, inc=1, device_id={"inner": mate}, device_id_type=MESH_ID)
+    greet(group, 1)
+    greet(other, 0)
+    pl.semaphore_wait(barrier, 2 * blocks - 1 + RING - 1)
+
+    def start_turn(k):
         mine = pl.ds(k * CHUNK, CHUNK)
         for s in range(1, RING):
             owner = lax.rem(ring + s, RING)
@@ -357,8 +359,13 @@
                 held.at[other, 0, chunk_rows(k), :, x_lanes(here)], cross_sem.at[0, k, here]
             )
 
+    for k in range(chunks):
+        start_turn(k)
+    for mate in mates:
+        pl.semaphore_signal(ready, inc=1, device_id={"inner": mate}, device_id_type=MESH_ID)
     send_halo(0)
     send_halo(1)
+    pl.semaphore_wait(ready, RING - 1)
     channelize(0)
     send_spectra(0)
     send_halo(2)
@@ -456,6 +463,7 @@
             pltpu.SemaphoreType.DMA,
             pltpu.SemaphoreType.DMA((chunks,)),
             pltpu.SemaphoreType.DMA((2,)),
+            pltpu.SemaphoreType.REGULAR,
         ],
         compiler_params=pltpu.CompilerParams(collective_id=0, has_side_effects=True),
     )(volts, coeffs, *tables())

time: 151 us -> 147 us (0.974)
  Pallas kernels: 147 us -> 142 us
    pallas_call x1, Pallas kernels: 147 us -> 142 us  [shards(): pl.pallas_call(whole_kernel, out_shape=(jax.ShapeDtypeStruct((2, inputs,...]
where the time goes in v5:
time: 147 us; the launch traced here: 146 us
  Pallas kernels  142 us (97%)
  other arithmetic  3.28 us (2%)
    pallas_call x1, Pallas kernels, shards(): pl.pallas_call(whole_kernel, out_shape=(jax.ShapeDtypeStruct((2, inputs,...  142 us
    mul x2, other arithmetic, shards(): return (autos[None] * scale, cross[None] * scale)  3.28 us

profile of v5, /device:TPU:17, one launch (start us, length us, event | category | flops | bytes accessed | tf_op | source)
XLA Modules:
  0.0 145.5 jit_solution(13365818108974111878)
XLA Ops:
  0.6 141.6 %shard_map.86 = (f32[2,384,384]{2,1,0:T(8,128)}, f32[2,192,384]{2,1,0:T(8,128)}) custom-call(bf16[384,32,128]{2,1,0:T(8,128)(2,1)} %bitcast.5, f32[3,16,128]{2,1,0:T(8,128)} %coeffs.1, bf16[256,256]{1,0:T(8,128)(2,1)} %constant.19.first, bf16[256,256]{1,0:T(8,128)(2,1)} %constant.20.second, bf16[256,256]{1,0:T(8,128)(2,1)} %constant.21.order, ...), custom_call_target="tpu_custom_call" | custom-call | tf_op jit(solution)/shard_map/pallas_call | solution.py:440
  142.3 0.0 copy-start
  142.3 2.4 %multiply_bitcast_fusion = f32[1,2,384,384]{3,2,1,0:T(8,128)} fusion(f32[2,384,384]{2,1,0:T(8,128)} %get-tuple-element.4), kind=kLoop, calls=%fused_computation | loop fusion | flops 294912 | bytes 2359296 | tf_op jit(solution)/shard_map/mul | solution.py:471
  144.7 0.0 copy-done
  144.7 0.9 multiply_bitcast_fusion.1
Async XLA Ops:
  142.3 2.4 %copy-start = (f32[2,192,384]{2,1,0:T(8,128)S(1)}, f32[2,192,384]{2,1,0:T(8,128)}, u32[]{:S(2)}) copy-start(f32[2,192,384]{2,1,0:T(8,128)} %get-tuple-element.5) | copy-start | bytes 1769476

commit v6 on v5

--- a/solution.py
+++ b/solution.py
@@ -377,12 +377,12 @@
     channelize(2)
     send_spectra(2)
     hand_on(1)
+    hand_on(2)
     for k in range(2):
         wait_own(0, k)
         wait_level(k)
     add_early(group, group, 0, autos)
     add_early(1, 0, 0, partial, half_lanes(met))
-    hand_on(2)
     for k in range(2):
         wait_own(near, k)
     add_early(1, 0, near, partial)

time: 147 us -> 148 us (level)
  no operation moved by 1% of the time
where the time goes in v6:
time: 148 us; the launch traced here: 146 us
  Pallas kernels  142 us (96%)
  other arithmetic  3.28 us (2%)
    pallas_call x1, Pallas kernels, shards(): pl.pallas_call(whole_kernel, out_shape=(jax.ShapeDtypeStruct((2, inputs,...  142 us
    mul x2, other arithmetic, shards(): return (autos[None] * scale, cross[None] * scale)  3.28 us

profile of v6, /device:TPU:17, one launch (start us, length us, event | category | flops | bytes accessed | tf_op | source)
XLA Modules:
  0.0 145.5 jit_solution(4159789899651688422)
XLA Ops:
  0.6 141.6 %shard_map.86 = (f32[2,384,384]{2,1,0:T(8,128)}, f32[2,192,384]{2,1,0:T(8,128)}) custom-call(bf16[384,32,128]{2,1,0:T(8,128)(2,1)} %bitcast.5, f32[3,16,128]{2,1,0:T(8,128)} %coeffs.1, bf16[256,256]{1,0:T(8,128)(2,1)} %constant.19.first, bf16[256,256]{1,0:T(8,128)(2,1)} %constant.20.second, bf16[256,256]{1,0:T(8,128)(2,1)} %constant.21.order, ...), custom_call_target="tpu_custom_call" | custom-call | tf_op jit(solution)/shard_map/pallas_call | solution.py:440
  142.3 0.0 copy-start
  142.3 2.4 %multiply_bitcast_fusion = f32[1,2,384,384]{3,2,1,0:T(8,128)} fusion(f32[2,384,384]{2,1,0:T(8,128)} %get-tuple-element.4), kind=kLoop, calls=%fused_computation | loop fusion | flops 294912 | bytes 2359296 | tf_op jit(solution)/shard_map/mul | solution.py:471
  144.7 0.0 copy-done
  144.7 0.9 multiply_bitcast_fusion.1
Async XLA Ops:
  142.3 2.4 %copy-start = (f32[2,192,384]{2,1,0:T(8,128)S(1)}, f32[2,192,384]{2,1,0:T(8,128)}, u32[]{:S(2)}) copy-start(f32[2,192,384]{2,1,0:T(8,128)} %get-tuple-element.5) | copy-start | bytes 1769476
